TPU v7x, 32 devices: a whole 2x2x4 slice. The times are simulated.
32 devices in a mesh: tiles: 2 (over y), strip: 4 (over z), col: 2 (over x), expo: 2 (over core).
Axes of the slice: x: 2, y: 2, z: 4, core: 2. Of those that a mesh axis runs over, the one named last changes fastest.
Arguments:
- mask_params: float32 [2, 2048, 256], P('expo', ('tiles', 'strip'), 'col'), parts along dimension 1, may hold values from -3 to 3
- target: int32 [2048, 256], P(('tiles', 'strip'), 'col'), parts along dimension 0, may hold values from 0 to 1, as said below
- col_taps: bfloat16 [24, 2, 65], replicated, may hold values from -0.75 to 0.75
- row_taps: bfloat16 [24, 2, 65], replicated, may hold values from -0.75 to 0.75
- kernel_weights: float32 [24], replicated, may hold values from 0.05 to 0.5
Outputs:
- new_params: float32 [2, 2048, 256], P('expo', ('tiles', 'strip'), 'col'), parts along dimension 1
- resist: float32 [2048, 256], P(('tiles', 'strip'), 'col'), parts along dimension 0
- mean_loss: float32 [2], P('tiles'), parts along dimension 0
There are 2 independent parts, one for each index of `tiles`. A program takes and returns all parts, laid end to end along the dimension named above; an argument that names none is the same for every part. Nothing has to cross between parts.
Inputs may be any that keep to these rules, and one draw needn't show every extreme that they name: `target`: 1 where the layout is printed, 0 elsewhere.
All inputs are finite; a program needn't handle non-finite values.
Results may differ from a plain program's by a relative error of at most 0.0078.
Values may be sent and summed in bfloat16 or wider, within the bound.
No kernel may reach another device: no remote copies, remote signals or barrier semaphores. Data moves between devices by JAX's collectives and lax.ppermute only.
A program may use at most 64 MiB of HBM per device.

v0:
```python
import jax
import jax.numpy as jnp
from jax import lax
from jax.sharding import PartitionSpec as P

HALF = 32
mask_slope = 4.0
resist_steep = 4.0
resist_level = 3.0
step_length = 0.5
norm_eps = 1e-06


def extended(array, sides, width):
    for axis, dim in sides:
        peers, length = (lax.axis_size(axis), array.shape[dim])
        up = [(i, (i + 1) % peers) for i in range(peers - 1)]
        down = [(j, i) for i, j in up]
        last = lax.slice_in_dim(array, length - width, length, axis=dim)
        first = lax.slice_in_dim(array, 0, width, axis=dim)
        before = lax.ppermute(last, axis, up)
        after = lax.ppermute(first, axis, down)
        array = jnp.concatenate([before, array, after], axis=dim)
    return array


def block_size():
    return 128


def toeplitz(tap_values, block_len):
    tap_count = tap_values.shape[-1]
    window_len = block_len + tap_count - 1
    padded_taps = jnp.concatenate(
        [tap_values, jnp.zeros(tap_values.shape[:-1] + (block_len,), tap_values.dtype)], axis=-1
    )
    repeated = jnp.tile(padded_taps, (1,) * (tap_values.ndim - 1) + (block_len,))
    return repeated[..., : block_len * window_len].reshape(
        tap_values.shape[:-1] + (block_len, window_len)
    )


def col_pass(source, tap_table):
    block_len, window_len = (tap_table.shape[1], tap_table.shape[2])
    length = source.shape[-1] - window_len + block_len
    windows = jnp.stack([source], axis=1)
    result = jnp.einsum("rnw,pow->prno", windows, tap_table, preferred_element_type=jnp.float32)
    return result.reshape(tap_table.shape[0], source.shape[0], length)


def row_pass(source, tap_table):
    block_len, window_len = (tap_table.shape[1], tap_table.shape[2])
    length = source.shape[1] - window_len + block_len
    windows = jnp.stack(
        [
            source[:, offset * block_len : offset * block_len + window_len, :]
            for offset in range(length // block_len)
        ],
        axis=1,
    )
    result = jnp.einsum("pnwc,qow->pqnoc", windows, tap_table, preferred_element_type=jnp.float32)
    return result.reshape(source.shape[0], tap_table.shape[0], length, source.shape[2])


def col_adjoint(source, tap_table):
    block_len, window_len = (tap_table.shape[1], tap_table.shape[2])
    length = source.shape[-1] - window_len + block_len
    windows = jnp.stack([source], axis=2)
    result = jnp.einsum("prnw,pow->rno", windows, tap_table, preferred_element_type=jnp.float32)
    return result.reshape(source.shape[1], length)


def shards(mask_params, target, col_taps, row_taps, kernel_weights):
    row_count, col_count = target.shape
    mask_field = jax.nn.sigmoid(mask_slope * mask_params[0])
    mask_half = mask_field.astype(jnp.bfloat16)
    col_block = block_size()
    row_block = block_size()
    mask_ext = extended(mask_half, (("strip", 0), ("col", 1)), HALF)

    def add_intensity(running, kernel):
        col_pair = col_taps[kernel]
        row_pair = row_taps[kernel]
        columns = col_pass(mask_ext, toeplitz(col_pair, col_block)).astype(jnp.bfloat16)
        pair_sums = row_pass(columns, toeplitz(row_pair, row_block))
        real_part = pair_sums[0, 0] - pair_sums[1, 1]
        imag_part = pair_sums[0, 1] + pair_sums[1, 0]
        updated = running + kernel_weights[kernel] * (real_part * real_part + imag_part * imag_part)
        return (updated, (real_part, imag_part))

    kernel_ids = jnp.arange(kernel_weights.shape[0], dtype=jnp.int32)
    zero_field = jnp.zeros((row_count, col_count), jnp.float32)
    intensity, stored = lax.scan(add_intensity, zero_field, kernel_ids)
    summed = lax.psum(intensity, "expo")
    resist = jax.nn.sigmoid(resist_steep * (summed - resist_level))
    mismatch = resist - target.astype(jnp.float32)
    pixels = row_count * col_count * lax.axis_size("strip") * lax.axis_size("col")
    loss_local = jnp.sum(mismatch * mismatch)
    loss_sum = lax.psum(loss_local, ("strip", "col"))
    slope_field = 2.0 * mismatch * resist_steep * resist * (1.0 - resist)

    def add_gradient(running, inputs):
        kernel, real_part, imag_part = inputs
        col_pair = col_taps[kernel]
        row_pair = row_taps[kernel]
        weighting = 2.0 * kernel_weights[kernel] * slope_field
        products = jnp.stack([weighting * real_part, weighting * imag_part]).astype(jnp.bfloat16)
        product_ext = extended(products, (("strip", 1),), HALF)
        returned = row_pass(product_ext, toeplitz(row_pair[:, ::-1], row_block))
        unrolled = jnp.stack(
            [returned[0, 0] + returned[1, 1], returned[1, 0] - returned[0, 1]]
        ).astype(jnp.bfloat16)
        unrolled_ext = extended(unrolled, (("col", 2),), HALF)
        return (running + col_adjoint(unrolled_ext, toeplitz(col_pair[:, ::-1], col_block)), None)

    descent, unused = lax.scan(add_gradient, zero_field, (kernel_ids, stored[0], stored[1]))
    gradient = descent * mask_slope * mask_field * (1.0 - mask_field)
    grad_squares = jnp.sum(gradient * gradient)
    square_sum = lax.psum(grad_squares, ("strip", "col", "expo"))
    root_mean = jnp.sqrt(square_sum / (lax.axis_size("expo") * pixels) + norm_eps)
    new_params = mask_params - step_length * gradient[None] / root_mean
    mean_loss = (loss_sum / pixels).reshape(1)
    return (new_params, resist, mean_loss)


def solution(mesh):
    return jax.shard_map(
        shards,
        mesh=mesh,
        in_specs=(
            P("expo", ("tiles", "strip"), "col"),
            P(("tiles", "strip"), "col"),
            P(),
            P(),
            P(),
        ),
        out_specs=(P("expo", ("tiles", "strip"), "col"), P(("tiles", "strip"), "col"), P("tiles")),
        check_vma=False,
    )
```

profile of v0, /device:TPU:0, one launch (start us, length us, event | category | flops | bytes accessed | tf_op | source)
XLA Modules:
  0.0 801.6 jit_solution(15718260283883890776)
XLA Ops:
  8.2 5.0 collective-permute-start.4
  28.8 172.5 %while.26 = (s32[]{:T(128)}, f32[256,128]{1,0:T(8,128)S(1)}, f32[24,256,128]{2,1,0:T(8,128)}, f32[24,256,128]{2,1,0:T(8,128)}, s32[24]{0:T(128)S(1)}, /*index=5*...) while((s32[]{:T(128)}, f32[256,128]{1,0:T(8,128)S(1)}, ...), condition=%wide.region_1.2_spmd.clone, body=%wide.region_0.1_spmd.clone.sunk | while | flops 82296832 | bytes 4555409 | solution.py:93
  202.0 17.4 %all-reduce.6.cloned.1.call-done = f32[256,128]{1,0:T(8,128)} async-done(((f32[256,128]{1,0:T(8,128)}), f32[256,128]{1,0:T(8,128)}) %all-reduce.6.cloned.1.call-update) | async-done | bytes 131088 | tf_op jit(solution)/shard_map/psum | solution.py:94
  221.7 521.3 %while.27 = (s32[]{:T(128)}, f32[256,128]{1,0:T(8,128)S(1)}, s32[24]{0:T(128)S(1)}, bf16[24,2,65]{2,1,0:T(2,128)(2,1)}, f32[24]{0:T(128)}, /*index=5*/f32[256,12...) while((s32[]{:T(128)}, f32[256,128]{1,0:T(8,128)S(1)}, ...), condition=%wide.region_4.5_spmd.clone, body=%wide.region_3.4_spmd.clone.sunk | while | flops 77824000 | bytes 7152573 | solution.py:116
  238.5 4.5 collective-permute-start.3
  261.5 4.5 collective-permute-start.3
  284.5 4.5 collective-permute-start.3
  306.0 4.5 collective-permute-start.3
  327.5 4.5 collective-permute-start.3
  349.0 4.5 collective-permute-start.3
  370.5 4.5 collective-permute-start.3
  392.1 4.5 collective-permute-start.3
  413.6 4.5 collective-permute-start.3
  435.1 4.5 collective-permute-start.3
  456.6 4.5 collective-permute-start.3
  478.3 4.5 collective-permute-start.3
  499.8 4.5 collective-permute-start.3
  521.3 4.5 collective-permute-start.3
  542.8 4.5 collective-permute-start.3
  564.3 4.5 collective-permute-start.3
  585.8 4.5 collective-permute-start.3
  607.4 4.5 collective-permute-start.3
  743.7 30.1 %psum.22 = f32[]{:T(128)} all-reduce(f32[]{:T(128)} %multiply_reduce_fusion.1), channel_id=1, replica_groups=mesh['tiles'=2,'strip'=4,'col'=2,'expo'=2] {'strip','col','expo'}, use_global_device_ids=true, to_apply=%region_6.7 | all-reduce | flops 1 | bytes 8 | tf_op jit(solution)/shard_map/psum | solution.py:119
  775.2 17.7 %psum.23 = f32[]{:T(128)} all-reduce(f32[]{:T(128)} %get-tuple-element.217), channel_id=1, replica_groups=mesh['tiles'=2,'strip'=4,'col'=2,'expo'=2] {'strip','col'}, use_global_device_ids=true, to_apply=%region_8.9 | all-reduce | flops 1 | bytes 8 | tf_op jit(solution)/shard_map/psum | solution.py:99
  (1359 shorter events, 517.0 us)
Async XLA Ops:
  7.2 212.2 %all-reduce.6.cloned.1.call-start = ((), (), s32[]{:S(2)}) async-start(), calls=%async_computation | async-start | bytes 262144 | tf_op jit(solution)/shard_map/psum | solution.py:94
  237.2 6.6 collective-permute-start.2
  260.2 6.6 collective-permute-start.2
  283.2 6.6 collective-permute-start.2
  304.7 6.6 collective-permute-start.2
  326.2 6.6 collective-permute-start.2
  347.7 6.6 collective-permute-start.2
  369.2 6.6 collective-permute-start.2
  390.8 6.6 collective-permute-start.2
  412.3 6.6 collective-permute-start.2
  433.8 6.6 collective-permute-start.2
  455.3 6.6 collective-permute-start.2
  477.0 6.6 collective-permute-start.2
  498.5 6.6 collective-permute-start.2
  520.0 6.6 collective-permute-start.2
  541.5 6.6 collective-permute-start.2
  563.0 6.6 collective-permute-start.2
  584.5 6.6 collective-permute-start.2
  606.1 6.6 collective-permute-start.2
  627.6 6.6 collective-permute-start.2
  649.1 6.6 collective-permute-start.2
  670.7 6.6 collective-permute-start.2
  692.2 6.6 collective-permute-start.2
  713.8 6.6 collective-permute-start.2
  (105 other events, 1284.2 us)
Sparse Core Ops, SparseCore 0:
  202.1 17.2 all-reduce.5
where the time goes:
time: 807 us; the launch traced here: 802 us
  starting transfers between devices  233 us (29%)
  local copies, waits for them, and re-layouts  185 us (23%)
  loops' own time  116 us (14%)
  waiting for transfers between devices  114 us (14%)
  other arithmetic  65.4 us (8%)
  blocking collectives  47.8 us (6%)
  matrix products  23.3 us (3%)
  between operations  16.7 us (2%)
    ppermute x50, starting transfers between devices, extended(): before = lax.ppermute(last, axis, up)  169 us
    ppermute x50, waiting for transfers between devices, extended(): after = lax.ppermute(first, axis, down)  77.3 us
    another operation x1, loops' own time, shards(): lax.scan(add_gradient, zero_field, (kernel_ids, stored[0], stored[1]))  67 us
    ppermute x50, starting transfers between devices, extended(): after = lax.ppermute(first, axis, down)  64.6 us
    another operation x1, loops' own time, shards(): intensity, stored = lax.scan(add_intensity, zero_field, kernel_ids)  48.9 us
    another operation x192, local copies, waits for them, and re-layouts, toeplitz(): jnp.tile(padded_taps, (1,) * (tap_values.ndim - 1) + (block_len,))  42.5 us
    psum x1, blocking collectives, shards(): square_sum = lax.psum(grad_squares, ('strip', 'col', 'expo'))  30.1 us
    dynamic_slice x24, local copies, waits for them, and re-layouts, add_gradient(): weighting = 2.0 * kernel_weights[kernel] * slope_field  29.8 us
  transfers between devices with their start and end apart: 101, of which 52 were waited for; matrix products, arithmetic and copies ran while one was open for 7% of the time, Pallas kernels for 0%

commit v1 on v0

--- a/solution.py
+++ b/solution.py
@@ -91,7 +91,7 @@
     kernel_ids = jnp.arange(kernel_weights.shape[0], dtype=jnp.int32)
     zero_field = jnp.zeros((row_count, col_count), jnp.float32)
     intensity, stored = lax.scan(add_intensity, zero_field, kernel_ids)
-    summed = lax.psum(intensity, "expo")
+    summed = jnp.sum(lax.all_gather(intensity, "expo"), axis=0)
     resist = jax.nn.sigmoid(resist_steep * (summed - resist_level))
     mismatch = resist - target.astype(jnp.float32)
     pixels = row_count * col_count * lax.axis_size("strip") * lax.axis_size("col")

time: 807 us -> 775 us (0.960)
  waiting for transfers between devices: 114 us -> 96.9 us
  between operations: 16.7 us -> 3.26 us
    psum x1 -> x0, waiting for transfers between devices: 17.4 us -> none  [shards(): summed = lax.psum(intensity, 'expo')]
  transfers between devices with their start and end apart: 101 -> 100, of which waited for: 52 -> 51; matrix products, arithmetic and copies ran while one was open for 7% -> 7% of each run, Pallas kernels for 0% -> 0%
where the time goes in v1:
time: 775 us; the launch traced here: 769 us
  starting transfers between devices  231 us (30%)
  local copies, waits for them, and re-layouts  184 us (24%)
  loops' own time  116 us (15%)
  waiting for transfers between devices  96.9 us (13%)
  other arithmetic  64.5 us (8%)
  blocking collectives  49.8 us (6%)
  matrix products  23.3 us (3%)
    ppermute x50, starting transfers between devices, extended(): before = lax.ppermute(last, axis, up)  167 us
    ppermute x50, waiting for transfers between devices, extended(): after = lax.ppermute(first, axis, down)  77.3 us
    another operation x1, loops' own time, shards(): lax.scan(add_gradient, zero_field, (kernel_ids, stored[0], stored[1]))  67 us
    ppermute x50, starting transfers between devices, extended(): after = lax.ppermute(first, axis, down)  64.6 us
    another operation x1, loops' own time, shards(): intensity, stored = lax.scan(add_intensity, zero_field, kernel_ids)  48.9 us
    another operation x192, local copies, waits for them, and re-layouts, toeplitz(): jnp.tile(padded_taps, (1,) * (tap_values.ndim - 1) + (block_len,))  42.5 us
    psum x1, blocking collectives, shards(): square_sum = lax.psum(grad_squares, ('strip', 'col', 'expo'))  30.1 us
    dynamic_slice x24, local copies, waits for them, and re-layouts, add_gradient(): weighting = 2.0 * kernel_weights[kernel] * slope_field  29.8 us
  transfers between devices with their start and end apart: 100, of which 51 were waited for; matrix products, arithmetic and copies ran while one was open for 7% of the time, Pallas kernels for 0%

profile of v1, /device:TPU:0, one launch (start us, length us, event | category | flops | bytes accessed | tf_op | source)
XLA Modules:
  0.0 769.4 jit_solution(14577342088156956495)
XLA Ops:
  1.6 5.0 collective-permute-start.4
  22.3 172.4 %while.26 = (s32[]{:T(128)}, f32[256,128]{1,0:T(8,128)S(1)}, f32[24,256,128]{2,1,0:T(8,128)}, f32[24,256,128]{2,1,0:T(8,128)}, s32[24]{0:T(128)S(1)}, /*index=5*...) while((s32[]{:T(128)}, f32[256,128]{1,0:T(8,128)S(1)}, ...), condition=%wide.region_1.2_spmd.clone, body=%wide.region_0.1_spmd.clone.sunk | while | flops 82296832 | bytes 4555409 | solution.py:93
  198.1 519.5 %while.27 = (s32[]{:T(128)}, f32[256,128]{1,0:T(8,128)S(1)}, s32[24]{0:T(128)S(1)}, bf16[24,2,65]{2,1,0:T(2,128)(2,1)}, f32[24]{0:T(128)}, /*index=5*/f32[256,12...) while((s32[]{:T(128)}, f32[256,128]{1,0:T(8,128)S(1)}, ...), condition=%wide.region_4.5_spmd.clone, body=%wide.region_3.4_spmd.clone.sunk | while | flops 77824000 | bytes 7152573 | solution.py:116
  214.7 4.5 collective-permute-start.3
  237.8 4.5 collective-permute-start.3
  259.3 4.5 collective-permute-start.3
  280.8 4.5 collective-permute-start.3
  302.4 4.5 collective-permute-start.3
  323.9 4.5 collective-permute-start.3
  345.4 4.5 collective-permute-start.3
  366.9 4.5 collective-permute-start.3
  388.4 4.5 collective-permute-start.3
  409.9 4.5 collective-permute-start.3
  431.5 4.5 collective-permute-start.3
  453.0 4.5 collective-permute-start.3
  474.5 4.5 collective-permute-start.3
  496.0 4.5 collective-permute-start.3
  517.6 4.5 collective-permute-start.3
  539.1 4.5 collective-permute-start.3
  560.6 4.5 collective-permute-start.3
  582.1 4.5 collective-permute-start.3
  603.6 4.5 collective-permute-start.3
  718.3 30.1 %psum.14 = f32[]{:T(128)} all-reduce(f32[]{:T(128)} %multiply_reduce_fusion.1), channel_id=1, replica_groups=mesh['tiles'=2,'strip'=4,'col'=2,'expo'=2] {'strip','col','expo'}, use_global_device_ids=true, to_apply=%region_6.7 | all-reduce | flops 1 | bytes 8 | tf_op jit(solution)/shard_map/psum | solution.py:119
  749.8 17.7 %psum.15 = f32[]{:T(128)} all-reduce(f32[]{:T(128)} %get-tuple-element.217), channel_id=1, replica_groups=mesh['tiles'=2,'strip'=4,'col'=2,'expo'=2] {'strip','col'}, use_global_device_ids=true, to_apply=%region_8.9 | all-reduce | flops 1 | bytes 8 | tf_op jit(solution)/shard_map/psum | solution.py:99
  (1356 shorter events, 511.0 us)
Async XLA Ops:
  213.4 6.6 collective-permute-start.2
  236.5 6.6 collective-permute-start.2
  258.0 6.6 collective-permute-start.2
  279.5 6.6 collective-permute-start.2
  301.1 6.6 collective-permute-start.2
  322.6 6.6 collective-permute-start.2
  344.1 6.6 collective-permute-start.2
  365.6 6.6 collective-permute-start.2
  387.1 6.6 collective-permute-start.2
  408.6 6.6 collective-permute-start.2
  430.2 6.6 collective-permute-start.2
  451.7 6.6 collective-permute-start.2
  473.2 6.6 collective-permute-start.2
  494.7 6.6 collective-permute-start.2
  516.3 6.6 collective-permute-start.2
  537.8 6.6 collective-permute-start.2
  559.3 6.6 collective-permute-start.2
  580.8 6.6 collective-permute-start.2
  602.3 6.6 collective-permute-start.2
  623.8 6.6 collective-permute-start.2
  645.3 6.6 collective-permute-start.2
  666.9 6.6 collective-permute-start.2
  688.4 6.6 collective-permute-start.2
  709.9 6.6 collective-permute-start.2
  (103 other events, 1257.2 us)
